TPU v7x, 32 devices: a whole 2x2x4 slice. The times are simulated.
32 devices in a mesh: kv: 4 (over y, x), seq: 8 (over z, core).
Axes of the slice: x: 2, y: 2, z: 4, core: 2. Of those that a mesh axis runs over, the one named last changes fastest.
Arguments:
- queries: bfloat16 [1024, 12288], P('seq', 'kv'), may hold values from -400 to 400
- cache_keys: bfloat16 [8192, 768], P('seq', 'kv'), may hold values from -6 to 6
- cache_values: bfloat16 [8192, 512], P('seq', 'kv'), may hold values from -6 to 6
- incoming_keys: bfloat16 [1024, 768], P('seq', 'kv'), may hold values from -6 to 6
- new_values: bfloat16 [1024, 512], P('seq', 'kv'), may hold values from -6 to 6
- comp_key_weight: bfloat16 [6144, 192], P('kv'), may hold values from -0.078125 to 0.078125
- comp_value_weight: bfloat16 [4096, 128], P('kv'), may hold values from -0.09375 to 0.09375
- select_blocks: int32 [32, 4, 16], P('seq', 'kv'), may hold values from 0 to 127, as said below
- gate_weight: bfloat16 [64, 192, 3], P('kv'), may hold values from -0.4375 to 0.4375
Outputs:
- attended: bfloat16 [1024, 8192], P('seq', 'kv')
Inputs may be any that keep to these rules, and one draw needn't show every extreme that they name: `select_blocks`: each row names 16 different blocks. For each KV group, the rows of one device of seq (4 tiles) name blocks of any one cache shard (the 16 blocks of one index of seq) at most 16 times in all, and in every draw the rows of every device name one shard's blocks exactly 16 times.
All inputs are finite; a program needn't handle non-finite values.
Results may differ from a plain program's by a relative error of at most 0.012.
Values may be sent and summed in bfloat16 or wider, within the bound.
A program may use at most 128 MiB of HBM per device.

v0:
```python
import jax
import jax.numpy as jnp
from jax import lax
from jax.sharding import PartitionSpec as P

CMP_STRIDE = 16
SEL_BLOCK = 64
WINDOW = 512
MASKED = -1e30


def passed_along(block, axis, distance):
    devices = range(lax.axis_size(axis))
    route = [((i - distance) % len(devices), i) for i in devices]
    return lax.ppermute(block, axis, route)


def from_behind(x, axis, by):
    peers = lax.axis_size(axis)
    pairs = [(i, i + by) for i in range(peers) if 0 <= i + by < peers]
    return lax.ppermute(x, axis, pairs)


def pack_rows(keys, values):
    return jnp.concatenate([keys.reshape(-1), values.reshape(-1)])


def unpack_rows(flat, count, key_width, value_width):
    keys = flat[: count * key_width].reshape(count, key_width)
    values = flat[count * key_width : count * (key_width + value_width)].reshape(count, value_width)
    return (keys, values)


def finish_rows(scores, values):
    top = jnp.max(scores, axis=-1, keepdims=True)
    weights = jnp.exp(scores - top)
    total = jnp.sum(weights, axis=-1, keepdims=True)
    mixed = jnp.matmul(weights.astype(jnp.bfloat16), values, preferred_element_type=jnp.float32)
    return mixed / total


def shards(
    queries,
    cache_keys,
    cache_values,
    incoming_keys,
    new_values,
    comp_key_weight,
    comp_value_weight,
    select_blocks,
    gate_weight,
):
    heads, key_width, _ = gate_weight.shape
    value_width = cache_values.shape[1]
    query_count = queries.shape[0]
    cache_count = cache_keys.shape[0]
    ranks = lax.axis_size("seq")
    place = lax.axis_index("seq")
    scale = key_width ** (-0.5)
    rows = queries.reshape(query_count * heads, key_width)
    row_total = rows.shape[0]
    stretch_pos = place * query_count + jnp.arange(query_count, dtype=jnp.int32)
    lookback_length = -(-WINDOW // query_count)
    weight_keys, weight_values = (
        lax.all_gather(comp_key_weight, "kv", axis=0, tiled=True),
        lax.all_gather(comp_value_weight, "kv", axis=0, tiled=True),
    )
    tail_pack = pack_rows(cache_keys[cache_count - WINDOW :], cache_values[cache_count - WINDOW :])
    moved_tail = passed_along(tail_pack, "seq", 1)
    before_keys, before_values = unpack_rows(moved_tail, WINDOW, key_width, value_width)
    edge_keys = before_keys[WINDOW - CMP_STRIDE :]
    edge_values = before_values[WINDOW - CMP_STRIDE :]
    held_tail = jnp.where(place == 0, moved_tail, jnp.zeros_like(moved_tail))
    tail_size = held_tail.shape[0]
    tail_flat = held_tail
    near_keys = []
    near_values = []
    nearby_positions = []
    near_valid = []
    own = pack_rows(incoming_keys, new_values)
    own_size = own.shape[0]
    for back in range(lookback_length, 0, -1):
        moved = from_behind(jnp.concatenate([own, held_tail]), "seq", back)
        got_keys, got_values = unpack_rows(moved, query_count, key_width, value_width)
        tail_flat = jnp.where(place == back, moved[own_size : own_size + tail_size], tail_flat)
        near_keys.append(got_keys)
        near_values.append(got_values)
        nearby_positions.append(
            (place - back) * query_count + jnp.arange(query_count, dtype=jnp.int32)
        )
        near_valid.append(jnp.broadcast_to(place >= back, (query_count,)))
    tail_keys, tail_values = unpack_rows(tail_flat, WINDOW, key_width, value_width)
    near_keys.append(tail_keys)
    near_values.append(tail_values)
    nearby_positions.append(jnp.arange(WINDOW, dtype=jnp.int32) - WINDOW)
    near_valid.append(jnp.ones((WINDOW,), dtype=bool))
    near_keys.append(incoming_keys)
    near_values.append(new_values)
    nearby_positions.append(stretch_pos)
    near_valid.append(jnp.ones((query_count,), dtype=bool))
    half_keys = CMP_STRIDE * key_width
    half_values = CMP_STRIDE * value_width
    lead_keys = jnp.concatenate([edge_keys, cache_keys[: cache_count - CMP_STRIDE]]).reshape(
        -1, half_keys
    )
    lead_values = jnp.concatenate([edge_values, cache_values[: cache_count - CMP_STRIDE]]).reshape(
        -1, half_values
    )
    comp_keys = (
        jnp.dot(lead_keys, weight_keys[:half_keys], preferred_element_type=jnp.float32)
        + jnp.dot(
            cache_keys.reshape(-1, half_keys),
            weight_keys[half_keys:],
            preferred_element_type=jnp.float32,
        )
    ).astype(jnp.bfloat16)
    comp_values = (
        jnp.dot(lead_values, weight_values[:half_values], preferred_element_type=jnp.float32)
        + jnp.dot(
            cache_values.reshape(-1, half_values),
            weight_values[half_values:],
            preferred_element_type=jnp.float32,
        )
    ).astype(jnp.bfloat16)
    start = jnp.int32(0)
    top = jnp.full((row_total,), MASKED, jnp.float32)
    total = jnp.zeros((row_total,), jnp.float32)
    summed = jnp.zeros((row_total, value_width), jnp.float32)
    keys = lax.all_gather(comp_keys, "seq", axis=0, tiled=True)
    values = lax.all_gather(comp_values, "seq", axis=0, tiled=True)
    length = keys.shape[0]
    block = length
    for size in (1024, 512, 256, 128):
        if length % size == 0:
            block = size
            break
    for index in range(length // block):
        key_block = keys[index * block : (index + 1) * block]
        value_block = values[index * block : (index + 1) * block]
        scores = (
            jnp.einsum("rd,kd->rk", rows, key_block, preferred_element_type=jnp.float32) * scale
        )
        key_at = start + index * block + jnp.arange(block, dtype=jnp.int32)
        scores = jnp.where(key_at[None, :] > 0, scores, MASKED)
        newtop = jnp.maximum(top, jnp.max(scores, axis=1))
        factor = jnp.exp(top - newtop)
        weights = jnp.exp(scores - newtop[:, None])
        total = total * factor + jnp.sum(weights, axis=1)
        summed = summed * factor[:, None] + jnp.dot(
            weights.astype(jnp.bfloat16), value_block, preferred_element_type=jnp.float32
        )
        top = newtop
    top, total, summed = (top, total, summed)
    compressed_out = summed / total[:, None]
    chosen = select_blocks.reshape(-1)
    shard_blocks = cache_count // SEL_BLOCK
    capacity = max(2, 2 * chosen.shape[0] // ranks)
    owner = chosen // shard_blocks
    local = chosen - owner * shard_blocks
    onehot = (owner[:, None] == jnp.arange(ranks, dtype=jnp.int32)[None, :]).astype(jnp.int32)
    position = jnp.sum((jnp.cumsum(onehot, axis=0) - 1) * onehot, axis=1)
    request = jnp.full((ranks, capacity), -1, jnp.int32).at[owner, position].set(local)
    key_blocks = cache_keys.reshape(shard_blocks, SEL_BLOCK, key_width)
    value_block_list = cache_values.reshape(shard_blocks, SEL_BLOCK, value_width)
    safe = jnp.clip(
        lax.all_to_all(request, "seq", split_axis=0, concat_axis=0, tiled=True), 0, shard_blocks - 1
    )
    got_keys = lax.all_to_all(key_blocks[safe], "seq", split_axis=0, concat_axis=0, tiled=True)
    got_values = lax.all_to_all(
        value_block_list[safe], "seq", split_axis=0, concat_axis=0, tiled=True
    )
    where_at = owner * capacity + position
    tile_count = select_blocks.shape[0]
    gathered_keys = got_keys.reshape(ranks * capacity, SEL_BLOCK, key_width)[where_at]
    picked_values = got_values.reshape(ranks * capacity, SEL_BLOCK, value_width)[where_at]
    gathered_keys, picked_values = (
        gathered_keys.reshape(tile_count, -1, key_width),
        picked_values.reshape(tile_count, -1, value_width),
    )
    tile_count = gathered_keys.shape[0]
    tile_row_count = rows.reshape(tile_count, -1, key_width)
    tile_scores = (
        jnp.einsum(
            "izu,ixu->izx", tile_row_count, gathered_keys, preferred_element_type=jnp.float32
        )
        * scale
    )
    selected_out = finish_rows(tile_scores, picked_values).reshape(row_total, value_width)
    context_keys = jnp.concatenate(near_keys)
    context_values = jnp.concatenate(near_values)
    context_positions = jnp.concatenate(nearby_positions)
    context_valid = jnp.concatenate(near_valid)
    sliding_scores = (
        jnp.einsum("rd,kd->rk", rows, context_keys, preferred_element_type=jnp.float32) * scale
    )
    allowed = (
        context_valid[None, :]
        & (context_positions[None, :] <= stretch_pos[:, None])
        & (context_positions[None, :] > stretch_pos[:, None] - WINDOW)
    )
    sliding_scores = jnp.where(
        allowed[:, None, :], sliding_scores.reshape(query_count, heads, -1), MASKED
    )
    window_out = finish_rows(sliding_scores.reshape(row_total, -1), context_values)
    logits = jnp.einsum(
        "thd,hdb->thb",
        queries.reshape(query_count, heads, key_width),
        gate_weight,
        preferred_element_type=jnp.float32,
    )
    gates = jax.nn.sigmoid(logits)
    mixed = (
        gates[:, :, 0:1] * compressed_out.reshape(query_count, heads, value_width)
        + gates[:, :, 1:2] * selected_out.reshape(query_count, heads, value_width)
        + gates[:, :, 2:3] * window_out.reshape(query_count, heads, value_width)
    )
    return mixed.astype(jnp.bfloat16).reshape(query_count, heads * value_width)


def solution(mesh):
    placed = (
        P("seq", "kv"),
        P("seq", "kv"),
        P("seq", "kv"),
        P("seq", "kv"),
        P("seq", "kv"),
        P("kv", None),
        P("kv", None),
        P("seq", "kv", None),
        P("kv", None, None),
    )
    return jax.shard_map(
        shards, mesh=mesh, in_specs=placed, out_specs=P("seq", "kv"), check_vma=False
    )
```

profile of v0, /device:TPU:0, one launch (start us, length us, event | category | flops | bytes accessed | tf_op | source)
XLA Modules:
  0.0 310.4 jit_solution(10423262976556319975)
XLA Ops:
  14.6 10.2 %scatter_fusion = s32[8,16]{1,0:T(8,128)} fusion(s32[8,16]{1,0:T(8,128)} %broadcast_in_dim.83, s32[64]{0:T(128)S(1)} %fusion.59, s32[64]{0:T(128)S(1)} %get-tuple-element.7), kind=kCustom, calls=%fused_computation.4 | custom fusion | bytes 1280 | tf_op jit(solution)/shard_map/scatter | solution.py:162
  24.7 6.3 %all-to-all-start = ((s32[8,1,16]{2,1,0:T(1,128)}), s32[8,1,16]{2,1,0:T(1,128)}, u32[]{:S(2)}, u32[]{:S(2)}) async-start(s32[8,1,16]{2,1,0:T(1,128)} %bitcast.10), calls=%async_computation | async-start | bytes 8192 | tf_op jit(solution)/shard_map/all_to_all | solution.py:166
  32.0 2.1 reshape.394
  34.2 2.1 reshape_reshape.6
  43.5 2.5 copy.51
  47.3 1.4 copy.36
  50.9 2.8 gather_fusion
  53.7 2.2 gather_fusion.2
  55.9 5.1 %all-to-all-start.2 = ((bf16[8,16,64,128]{3,2,1,0:T(8,128)(2,1)}), bf16[8,16,64,128]{3,2,1,0:T(8,128)(2,1)}, u32[]{:S(2)}, u32[]{:S(2)}) async-start(bf16[8,16,64,128]{3,2,1,0:T(8,128)(2,1)} %bitcast.113), calls=%async_computation.2 | async-start | bytes 4194304 | tf_op jit(solution)/shard_map/all_to_all | solution.py:169
  62.8 4.6 %collective-permute-start.1 = (bf16[204800]{0:T(1024)(128)(2,1)}, bf16[204800]{0:T(1024)(128)(2,1)}, u32[]{:S(2)}, u32[]{:S(2)}) collective-permute-start(bf16[204800]{0:T(1024)(128)(2,1)} %pad_maximum_fusion), channel_id=1, source_target_pairs={{0,4},{1,5},{2,6},{3,7},{8,12},{9,13},{10,14},{11,15},{16,20},{17,... | collective-permute-start | bytes 1228808 | tf_op jit(solution)/shard_map/ppermute | solution.py:21
  67.4 3.6 %collective-permute-start.2 = (bf16[204800]{0:T(1024)(128)(2,1)}, bf16[204800]{0:T(1024)(128)(2,1)}, u32[]{:S(2)}, u32[]{:S(2)}) collective-permute-start(bf16[204800]{0:T(1024)(128)(2,1)} %pad_maximum_fusion), channel_id=1, source_target_pairs={{0,3},{1,4},{2,5},{3,6},{4,7},{8,11},{9,12},{10,13},{11,14},{12,15... | collective-permute-start | bytes 1228808 | tf_op jit(solution)/shard_map/ppermute | solution.py:21
  71.0 2.6 collective-permute-start.3
  73.6 2.1 collective-permute-start.4
  81.9 23.0 %collective-permute-done.1 = bf16[204800]{0:T(1024)(128)(2,1)} collective-permute-done((bf16[204800]{0:T(1024)(128)(2,1)}, bf16[204800]{0:T(1024)(128)(2,1)}, u32[]{:S(2)}, u32[]{:S(2)}) %collective-permute-start.1) | collective-permute-done | bytes 409632 | tf_op jit(solution)/shard_map/ppermute | solution.py:21
  106.3 7.4 %collective-permute-done.2 = bf16[204800]{0:T(1024)(128)(2,1)} collective-permute-done((bf16[204800]{0:T(1024)(128)(2,1)}, bf16[204800]{0:T(1024)(128)(2,1)}, u32[]{:S(2)}, u32[]{:S(2)}) %collective-permute-start.2) | collective-permute-done | bytes 409632 | tf_op jit(solution)/shard_map/ppermute | solution.py:21
  115.0 7.4 %collective-permute-done.3 = bf16[204800]{0:T(1024)(128)(2,1)} collective-permute-done((bf16[204800]{0:T(1024)(128)(2,1)}, bf16[204800]{0:T(1024)(128)(2,1)}, u32[]{:S(2)}, u32[]{:S(2)}) %collective-permute-start.3) | collective-permute-done | bytes 409632 | tf_op jit(solution)/shard_map/ppermute | solution.py:21
  122.5 1.4 fusion.49
  130.5 33.3 %all-to-all-start.1 = ((bf16[8,16,64,192]{3,2,1,0:T(8,128)(2,1)}), bf16[8,16,64,192]{3,2,1,0:T(8,128)(2,1)}, u32[]{:S(2)}, u32[]{:S(2)}) async-start(bf16[8,16,64,192]{3,2,1,0:T(8,128)(2,1)} %bitcast.110), calls=%async_computation.1 | async-start | bytes 8388608 | tf_op jit(solution)/shard_map/all_to_all | solution.py:168
  164.4 1.4 constant_dynamic-update-slice_fusion.7
  165.8 3.2 %fusion.65 = (f32[2048]{0:T(1024)S(1)}, f32[2048,1152]{0,1:T(8,128)S(1)}) fusion(pred[2048,1152]{0,1:T(32,128)(4,1)S(1)} %copy.51, bf16[1152,192]{1,0:T(8,128)(2,1)S(1)} %constant_dynamic-update-slice_fusion.1, bf16[2048,192]{1,0:T(8,128)(2,1)} %reshape.394), kind=kOutput, calls=%fused_computation.126 | convolution fusion | flops 913045504 | bytes 13033472 | tf_op jit(solution)/shard_map/rd,kd->rk/dot_general | solution.py:194
  170.4 1.8 fusion.16
  176.0 88.1 %all_gather.15 = bf16[512,128]{1,0:T(8,128)(2,1)S(1)} all-gather(bf16[64,128]{1,0:T(8,128)(2,1)S(1)} %fusion.37), channel_id=1, replica_groups=mesh['kv'=4,'seq'=8] {'seq'}, dimensions={0}, use_global_device_ids=true | all-gather | bytes 147456 | tf_op jit(solution)/shard_map/all_gather | solution.py:130
  264.1 1.8 fusion.23
  265.9 1.9 fusion.30
  267.8 14.4 %all_gather.13 = bf16[512,192]{1,0:T(8,128)(2,1)S(1)} all-gather(bf16[64,192]{1,0:T(8,128)(2,1)S(1)} %fusion.30), channel_id=1, replica_groups=mesh['kv'=4,'seq'=8] {'seq'}, dimensions={0}, use_global_device_ids=true | all-gather | bytes 221184 | tf_op jit(solution)/shard_map/all_gather | solution.py:129
  284.0 1.5 fusion.15
  286.7 3.4 %gather_fusion.3 = bf16[64,64,128]{2,1,0:T(8,128)(2,1)} fusion(bf16[128,64,128]{2,1,0:T(8,128)(2,1)} %bitcast.20, s32[1024]{0:T(1024)} %pad_clamp_fusion), kind=kCustom, calls=%fused_computation.3 | custom fusion | bytes 2097408 | tf_op jit(solution)/shard_map/gather | solution.py:175
  290.1 3.0 gather_fusion.1
  294.4 1.4 fusion.3
  295.8 3.2 %fusion.41 = f32[4,512,128]{2,1,0:T(8,128)} fusion(bf16[4,1024,128]{2,1,0:T(8,128)(2,1)S(1)} %bitcast.119, f32[4,1024,512]{2,1,0:T(8,128)S(1)} %get-tuple-element.17, f32[4,512]{1,0:T(4,128)S(1)} %get-tuple-element.16, f32[4,512]{1,0:T(4,128)S(1)} %fusion.3), kind=kOutput, calls=%fused_computation.50 | convolution fusion | flops 543424512 | bytes 10502144 | tf_op jit(solution)/shard_map/dot_general | solution.py:38
  299.0 1.5 reshape_reshape.7
  301.6 1.9 fusion.39
  (153 shorter events, 47.7 us)
Async XLA Ops:
  6.5 25.3 %copy-start.6 = (bf16[1024,192]{0,1:T(8,128)(2,1)S(1)}, bf16[1024,192]{0,1:T(8,128)(2,1)}, u32[]{:S(2)}) copy-start(bf16[1024,192]{0,1:T(8,128)(2,1)} %param.10) | copy-start | bytes 1179652
  6.5 25.5 %copy-start.1 = (bf16[128,3072]{1,0:T(8,128)(2,1)S(1)}, bf16[128,3072]{1,0:T(8,128)(2,1)}, u32[]{:S(2)}) copy-start(bf16[128,3072]{1,0:T(8,128)(2,1)} %param.9) | copy-start | bytes 2359300
  6.5 166.9 %all-gather.5.cloned.1.call-start = ((), (), s32[]{:S(2)}) async-start(), calls=%async_computation.4 | async-start | bytes 1310720 | tf_op jit(solution)/shard_map/all_gather | solution.py:66
  10.3 28.9 %copy-start.18 = (bf16[16,192,3]{1,0,2:T(8,128)(2,1)S(1)}, bf16[16,192,3]{1,0,2:T(8,128)(2,1)}, u32[]{:S(2)}) copy-start(bf16[16,192,3]{1,0,2:T(8,128)(2,1)} %param.17) | copy-start | bytes 55300
  10.3 50.6 %collective-permute-start = (bf16[163840]{0:T(1024)(128)(2,1)}, bf16[163840]{0:T(1024)(128)(2,1)}, u32[]{:S(2)}, u32[]{:S(2)}) collective-permute-start(bf16[163840]{0:T(1024)(128)(2,1)} %pad_maximum_fusion.2), channel_id=1, source_target_pairs={{7,0},{0,1},{1,2},{2,3},{3,4},{4,5},{5,6},{6,7},{15,8},{8,9},{9,10... | collective-permute-start | bytes 983048 | tf_op jit(solution)/shard_map/ppermute | solution.py:15
  24.7 15.7 %copy-start = (bf16[1024,128]{1,0:T(8,128)(2,1)S(1)}, bf16[1024,128]{1,0:T(8,128)(2,1)}, u32[]{:S(2)}) copy-start(bf16[1024,128]{1,0:T(8,128)(2,1)} %param.11) | copy-start | bytes 786436
  24.7 25.5 %all-to-all-start = ((s32[8,1,16]{2,1,0:T(1,128)}), s32[8,1,16]{2,1,0:T(1,128)}, u32[]{:S(2)}, u32[]{:S(2)}) async-start(s32[8,1,16]{2,1,0:T(1,128)} %bitcast.10), calls=%async_computation | async-start | bytes 8192 | tf_op jit(solution)/shard_map/all_to_all | solution.py:166
  31.0 233.1 %all-gather.3.cloned.1.call-start = ((), (), s32[]{:S(2)}) async-start(), calls=%async_computation.3 | async-start | bytes 2949120 | tf_op jit(solution)/shard_map/all_gather | solution.py:65
  31.7 10.3 %copy-start.17 = (bf16[128,192]{0,1:T(8,128)(2,1)S(1)}, bf16[128,192]{0,1:T(8,128)(2,1)}, u32[]{:S(2)}) copy-start(bf16[128,192]{0,1:T(8,128)(2,1)} %param.12) | copy-start | bytes 147460
  42.1 1.4 copy-start.9
  53.7 8.3 %copy-start.15 = (bf16[24576]{0:T(1024)(128)(2,1)S(1)}, bf16[24576]{0:T(1024)(128)(2,1)}, u32[]{:S(2)}) copy-start(bf16[24576]{0:T(1024)(128)(2,1)} %reshape.406) | copy-start | bytes 147460
  53.7 8.3 %copy-start.16 = (bf16[128,128]{1,0:T(8,128)(2,1)S(1)}, bf16[128,128]{1,0:T(8,128)(2,1)}, u32[]{:S(2)}) copy-start(bf16[128,128]{1,0:T(8,128)(2,1)} %param.13) | copy-start | bytes 98308
  55.9 74.6 %all-to-all-start.2 = ((bf16[8,16,64,128]{3,2,1,0:T(8,128)(2,1)}), bf16[8,16,64,128]{3,2,1,0:T(8,128)(2,1)}, u32[]{:S(2)}, u32[]{:S(2)}) async-start(bf16[8,16,64,128]{3,2,1,0:T(8,128)(2,1)} %bitcast.113), calls=%async_computation.2 | async-start | bytes 4194304 | tf_op jit(solution)/shard_map/all_to_all | solution.py:169
  62.8 42.1 %collective-permute-start.1 = (bf16[204800]{0:T(1024)(128)(2,1)}, bf16[204800]{0:T(1024)(128)(2,1)}, u32[]{:S(2)}, u32[]{:S(2)}) collective-permute-start(bf16[204800]{0:T(1024)(128)(2,1)} %pad_maximum_fusion), channel_id=1, source_target_pairs={{0,4},{1,5},{2,6},{3,7},{8,12},{9,13},{10,14},{11,15},{16,20},{17,... | collective-permute-start | bytes 1228808 | tf_op jit(solution)/shard_map/ppermute | solution.py:21
  67.4 46.3 %collective-permute-start.2 = (bf16[204800]{0:T(1024)(128)(2,1)}, bf16[204800]{0:T(1024)(128)(2,1)}, u32[]{:S(2)}, u32[]{:S(2)}) collective-permute-start(bf16[204800]{0:T(1024)(128)(2,1)} %pad_maximum_fusion), channel_id=1, source_target_pairs={{0,3},{1,4},{2,5},{3,6},{4,7},{8,11},{9,12},{10,13},{11,14},{12,15... | collective-permute-start | bytes 1228808 | tf_op jit(solution)/shard_map/ppermute | solution.py:21
  71.0 51.5 %collective-permute-start.3 = (bf16[204800]{0:T(1024)(128)(2,1)}, bf16[204800]{0:T(1024)(128)(2,1)}, u32[]{:S(2)}, u32[]{:S(2)}) collective-permute-start(bf16[204800]{0:T(1024)(128)(2,1)} %pad_maximum_fusion), channel_id=1, source_target_pairs={{0,2},{1,3},{2,4},{3,5},{4,6},{5,7},{8,10},{9,11},{10,12},{11,13},... | collective-permute-start | bytes 1228808 | tf_op jit(solution)/shard_map/ppermute | solution.py:21
  73.6 48.9 %collective-permute-start.4 = (bf16[204800]{0:T(1024)(128)(2,1)}, bf16[204800]{0:T(1024)(128)(2,1)}, u32[]{:S(2)}, u32[]{:S(2)}) collective-permute-start(bf16[204800]{0:T(1024)(128)(2,1)} %pad_maximum_fusion), channel_id=1, source_target_pairs={{0,1},{1,2},{2,3},{3,4},{4,5},{5,6},{6,7},{8,9},{9,10},{10,11},{11... | collective-permute-start | bytes 1228808 | tf_op jit(solution)/shard_map/ppermute | solution.py:21
  130.5 35.4 %copy-start.10 = (bf16[128,192]{1,0:T(8,128)(2,1)S(1)}, bf16[128,192]{1,0:T(8,128)(2,1)}, u32[]{:S(2)}) copy-start(bf16[128,192]{1,0:T(8,128)(2,1)} %copy-done.9) | copy-start | bytes 147460
  130.5 159.6 %all-to-all-start.1 = ((bf16[8,16,64,192]{3,2,1,0:T(8,128)(2,1)}), bf16[8,16,64,192]{3,2,1,0:T(8,128)(2,1)}, u32[]{:S(2)}, u32[]{:S(2)}) async-start(bf16[8,16,64,192]{3,2,1,0:T(8,128)(2,1)} %bitcast.110), calls=%async_computation.1 | async-start | bytes 8388608 | tf_op jit(solution)/shard_map/all_to_all | solution.py:168
  169.0 1.4 copy-start.19
  170.4 4.3 %copy-start.8 = (bf16[64,2048]{1,0:T(8,128)(2,1)S(1)}, bf16[64,2048]{1,0:T(8,128)(2,1)}, u32[]{:S(2)}) copy-start(bf16[64,2048]{1,0:T(8,128)(2,1)} %reshape.396) | copy-start | bytes 786436
  170.4 93.7 %copy-start.11 = (bf16[64,3072]{1,0:T(8,128)(2,1)S(1)}, bf16[64,3072]{1,0:T(8,128)(2,1)}, u32[]{:S(2)}) copy-start(bf16[64,3072]{1,0:T(8,128)(2,1)} %reshape.393) | copy-start | bytes 1179652
  172.2 109.9 %copy-start.3 = (bf16[2048,192]{1,0:T(8,128)(2,1)S(1)}, bf16[2048,192]{1,0:T(8,128)(2,1)}, u32[]{:S(2)}) copy-start(bf16[2048,192]{1,0:T(8,128)(2,1)} %reshape.394) | copy-start | bytes 2359300
  172.3 109.9 %copy-start.20 = (pred[512]{0:T(512)(128)(4,1)S(1)}, pred[512]{0:T(512)(128)(4,1)}, u32[]{:S(2)}) copy-start(pred[512]{0:T(512)(128)(4,1)} %iota_compare_fusion.1) | copy-start | bytes 1540
  285.5 7.6 %copy-start.2 = (bf16[4,512,192]{2,1,0:T(8,128)(2,1)S(1)}, bf16[4,512,192]{2,1,0:T(8,128)(2,1)}, u32[]{:S(2)}) copy-start(bf16[4,512,192]{2,1,0:T(8,128)(2,1)} %reshape_reshape.6) | copy-start | bytes 2359300
  294.4 1.4 copy-start.7
  295.8 4.7 %copy-start.12 = (f32[128,16]{1,0:T(8,128)S(1)}, f32[128,16]{1,0:T(8,128)}, u32[]{:S(2)}) copy-start(f32[128,16]{1,0:T(8,128)} %copy.36) | copy-start | bytes 24580
  295.8 5.1 %copy-start.13 = (f32[128,16]{1,0:T(8,128)S(1)}, f32[128,16]{1,0:T(8,128)}, u32[]{:S(2)}) copy-start(f32[128,16]{1,0:T(8,128)} %copy.41) | copy-start | bytes 24580
  299.0 2.2 copy-start.14
  299.0 2.6 copy-start.4
  299.0 2.6 copy-start.5
Sparse Core Ops, SparseCore 0:
  9.2 29.2 all-gather.4
  40.3 37.2 all-gather.2
where the time goes:
time: 312 us; the launch traced here: 310 us
  blocking collectives  103 us (33%)
  local copies, waits for them, and re-layouts  62.8 us (20%)
  starting transfers between devices  58.1 us (19%)
  waiting for transfers between devices  39.3 us (13%)
  matrix products  18.3 us (6%)
  other arithmetic  15.4 us (5%)
  between operations  14 us (4%)
    all_gather x1, blocking collectives, shards(): values = lax.all_gather(comp_values, 'seq', axis=0, tiled=True)  88.1 us
    ppermute x4, waiting for transfers between devices, from_behind(): return lax.ppermute(x, axis, pairs)  37.8 us
    all_to_all x1, starting transfers between devices, shards(): lax.all_to_all(key_blocks[safe], 'seq', split_axis=0, concat_axis=0, tile...  33.3 us
    all_gather x1, blocking collectives, shards(): keys = lax.all_gather(comp_keys, 'seq', axis=0, tiled=True)  14.4 us
    ppermute x4, starting transfers between devices, from_behind(): return lax.ppermute(x, axis, pairs)  12.9 us
    scatter x1, local copies, waits for them, and re-layouts, shards(): jnp.full((ranks, capacity), -1, jnp.int32).at[owner, position].set(local)  10.2 us
    unnamed x61, local copies, waits for them, and re-layouts  8.66 us
    all_to_all x1, starting transfers between devices, shards(): lax.all_to_all(request, 'seq', split_axis=0, concat_axis=0, tiled=True)  6.28 us
  transfers between devices with their start and end apart: 10, of which 3 were waited for; matrix products, arithmetic and copies ran while one was open for 27% of the time, Pallas kernels for 0%

commit v1 on v0

--- a/solution.py
+++ b/solution.py
@@ -127,7 +127,9 @@
     total = jnp.zeros((row_total,), jnp.float32)
     summed = jnp.zeros((row_total, value_width), jnp.float32)
     keys = lax.all_gather(comp_keys, "seq", axis=0, tiled=True)
-    values = lax.all_gather(comp_values, "seq", axis=0, tiled=True)
+    values = jnp.concatenate(
+        lax.all_to_all(jnp.stack([comp_values] * lax.axis_size("seq")), "seq", 0, 0), axis=0
+    )
     length = keys.shape[0]
     block = length
     for size in (1024, 512, 256, 128):

time: 312 us -> 294 us (0.942)
  blocking collectives: 103 us -> 79.3 us
  waiting for transfers between devices: 39.3 us -> 49.1 us
  starting transfers between devices: 58.1 us -> 51 us
    all_gather x1 -> x0, blocking collectives: 88.1 us -> none  [shards(): values = lax.all_gather(comp_values, 'seq', axis=0, tiled=True)]
    all_gather x1, blocking collectives: 14.4 us -> 79.3 us  [shards(): keys = lax.all_gather(comp_keys, 'seq', axis=0, tiled=True)]
    all_to_all x1, waiting for transfers between devices: 0.01 us -> 46.3 us  [shards(): lax.all_to_all(value_block_list[safe], 'seq', split_axis=0, concat_axis=0...]
    ppermute x4, waiting for transfers between devices: 37.8 us -> 0.01 us  [from_behind(): return lax.ppermute(x, axis, pairs)]
    all_to_all x1, starting transfers between devices: 33.3 us -> 4.69 us  [shards(): lax.all_to_all(key_blocks[safe], 'seq', split_axis=0, concat_axis=0, tile...]
    all_to_all x1, starting transfers between devices: 5.08 us -> 22.5 us  [shards(): lax.all_to_all(value_block_list[safe], 'seq', split_axis=0, concat_axis=0...]
    all_to_all x0 -> x1, starting transfers between devices: none -> 4.18 us  [shards(): lax.all_to_all(jnp.stack([comp_values] * lax.axis_size('seq')), 'seq', 0, 0)]
    unnamed x61 -> x59, local copies, waits for them, and re-layouts: 8.66 us -> 8.71 us
  transfers between devices with their start and end apart: 10 -> 11, of which waited for: 3 -> 2; matrix products, arithmetic and copies ran while one was open for 27% -> 29% of each run, Pallas kernels for 0% -> 0%
where the time goes in v1:
time: 294 us; the launch traced here: 292 us
  blocking collectives  79.3 us (27%)
  local copies, waits for them, and re-layouts  63 us (21%)
  starting transfers between devices  51 us (17%)
  waiting for transfers between devices  49.1 us (17%)
  matrix products  20.2 us (7%)
  other arithmetic  15.8 us (5%)
  between operations  14 us (5%)
    all_gather x1, blocking collectives, shards(): keys = lax.all_gather(comp_keys, 'seq', axis=0, tiled=True)  79.3 us
    all_to_all x1, waiting for transfers between devices, shards(): lax.all_to_all(value_block_list[safe], 'seq', split_axis=0, concat_axis=0...  46.3 us
    all_to_all x1, starting transfers between devices, shards(): lax.all_to_all(value_block_list[safe], 'seq', split_axis=0, concat_axis=0...  22.5 us
    ppermute x4, starting transfers between devices, from_behind(): return lax.ppermute(x, axis, pairs)  12.9 us
    scatter x1, local copies, waits for them, and re-layouts, shards(): jnp.full((ranks, capacity), -1, jnp.int32).at[owner, position].set(local)  10.2 us
    unnamed x59, local copies, waits for them, and re-layouts  8.71 us
    all_to_all x1, starting transfers between devices, shards(): lax.all_to_all(request, 'seq', split_axis=0, concat_axis=0, tiled=True)  6.14 us
    dot_general x2, matrix products, finish_rows(): jnp.matmul(weights.astype(jnp.bfloat16), values, preferred_element_type=j...  5.99 us
  transfers between devices with their start and end apart: 11, of which 2 were waited for; matrix products, arithmetic and copies ran while one was open for 29% of the time, Pallas kernels for 0%

profile of v1, /device:TPU:0, one launch (start us, length us, event | category | flops | bytes accessed | tf_op | source)
XLA Modules:
  0.0 292.5 jit_solution(4149696713774306006)
XLA Ops:
  14.5 10.2 %scatter_fusion = s32[8,16]{1,0:T(8,128)} fusion(s32[8,16]{1,0:T(8,128)} %broadcast_in_dim.83, s32[64]{0:T(128)S(1)} %fusion.59, s32[64]{0:T(128)S(1)} %get-tuple-element.7), kind=kCustom, calls=%fused_computation.4 | custom fusion | bytes 1280 | tf_op jit(solution)/shard_map/scatter | solution.py:164
  24.7 6.1 %all-to-all-start.1 = ((s32[8,1,16]{2,1,0:T(1,128)}), s32[8,1,16]{2,1,0:T(1,128)}, u32[]{:S(2)}, u32[]{:S(2)}) async-start(s32[8,1,16]{2,1,0:T(1,128)} %bitcast.11), calls=%async_computation.1 | async-start | bytes 8192 | tf_op jit(solution)/shard_map/all_to_all | solution.py:168
  31.9 2.1 reshape.399
  34.0 2.1 reshape_reshape.6
  42.4 2.5 copy.51
  46.3 1.4 copy.36
  50.9 1.6 pad_maximum_fusion
  52.5 4.6 %collective-permute-start.1 = (bf16[204800]{0:T(1024)(128)(2,1)}, bf16[204800]{0:T(1024)(128)(2,1)}, u32[]{:S(2)}, u32[]{:S(2)}) collective-permute-start(bf16[204800]{0:T(1024)(128)(2,1)} %pad_maximum_fusion), channel_id=1, source_target_pairs={{0,4},{1,5},{2,6},{3,7},{8,12},{9,13},{10,14},{11,15},{16,20},{17,... | collective-permute-start | bytes 1228808 | tf_op jit(solution)/shard_map/ppermute | solution.py:21
  57.1 3.6 %collective-permute-start.2 = (bf16[204800]{0:T(1024)(128)(2,1)}, bf16[204800]{0:T(1024)(128)(2,1)}, u32[]{:S(2)}, u32[]{:S(2)}) collective-permute-start(bf16[204800]{0:T(1024)(128)(2,1)} %pad_maximum_fusion), channel_id=1, source_target_pairs={{0,3},{1,4},{2,5},{3,6},{4,7},{8,11},{9,12},{10,13},{11,14},{12,15... | collective-permute-start | bytes 1228808 | tf_op jit(solution)/shard_map/ppermute | solution.py:21
  60.7 2.6 collective-permute-start.3
  63.3 2.1 collective-permute-start.4
  71.2 4.2 %all-to-all-start = ((bf16[8,64,128]{2,1,0:T(8,128)(2,1)}), bf16[8,64,128]{2,1,0:T(8,128)(2,1)}, u32[]{:S(2)}, u32[]{:S(2)}) async-start(bf16[8,64,128]{2,1,0:T(8,128)(2,1)} %stack.2), calls=%async_computation | async-start | bytes 262144 | tf_op jit(solution)/shard_map/all_to_all | solution.py:131
  75.4 2.8 gather_fusion
  78.2 2.2 gather_fusion.2
  84.7 1.4 all-to-all-done
  86.1 22.5 %all-to-all-start.3 = ((bf16[8,16,64,128]{3,2,1,0:T(8,128)(2,1)}), bf16[8,16,64,128]{3,2,1,0:T(8,128)(2,1)}, u32[]{:S(2)}, u32[]{:S(2)}) async-start(bf16[8,16,64,128]{3,2,1,0:T(8,128)(2,1)} %bitcast.114), calls=%async_computation.3 | async-start | bytes 4194304 | tf_op jit(solution)/shard_map/all_to_all | solution.py:171
  108.7 1.5 fusion.49
  111.5 46.3 %all-to-all-done.3 = bf16[8,16,64,128]{3,2,1,0:T(8,128)(2,1)} async-done(((bf16[8,16,64,128]{3,2,1,0:T(8,128)(2,1)}), bf16[8,16,64,128]{3,2,1,0:T(8,128)(2,1)}, u32[]{:S(2)}, u32[]{:S(2)}) %all-to-all-start.3) | async-done | bytes 2097184 | tf_op jit(solution)/shard_map/all_to_all | solution.py:171
  157.8 4.7 %all-to-all-start.2 = ((bf16[8,16,64,192]{3,2,1,0:T(8,128)(2,1)}), bf16[8,16,64,192]{3,2,1,0:T(8,128)(2,1)}, u32[]{:S(2)}, u32[]{:S(2)}) async-start(bf16[8,16,64,192]{3,2,1,0:T(8,128)(2,1)} %bitcast.111), calls=%async_computation.2 | async-start | bytes 8388608 | tf_op jit(solution)/shard_map/all_to_all | solution.py:170
  162.5 1.4 fusion.53
  167.7 1.4 fusion.52
  171.9 3.2 %fusion.65 = (f32[2048]{0:T(1024)S(1)}, f32[2048,1152]{0,1:T(8,128)S(1)}) fusion(pred[2048,1152]{0,1:T(32,128)(4,1)S(1)} %copy.51, bf16[1152,192]{1,0:T(8,128)(2,1)S(1)} %constant_dynamic-update-slice_fusion.1, bf16[2048,192]{1,0:T(8,128)(2,1)} %reshape.399), kind=kOutput, calls=%fused_computation.126 | convolution fusion | flops 913045504 | bytes 13033472 | tf_op jit(solution)/shard_map/rd,kd->rk/dot_general | solution.py:196
  176.4 2.8 fusion.16
  180.4 1.8 fusion.23
  182.2 1.8 fusion.30
  184.0 79.3 %all_gather.10 = bf16[512,192]{1,0:T(8,128)(2,1)S(1)} all-gather(bf16[64,192]{1,0:T(8,128)(2,1)S(1)} %fusion.30), channel_id=1, replica_groups=mesh['kv'=4,'seq'=8] {'seq'}, dimensions={0}, use_global_device_ids=true | all-gather | bytes 221184 | tf_op jit(solution)/shard_map/all_gather | solution.py:129
  265.1 2.4 fusion.15
  268.7 3.5 %gather_fusion.3 = bf16[64,64,128]{2,1,0:T(8,128)(2,1)} fusion(bf16[128,64,128]{2,1,0:T(8,128)(2,1)} %bitcast.21, s32[1024]{0:T(1024)} %pad_clamp_fusion), kind=kCustom, calls=%fused_computation.3 | custom fusion | bytes 2097408 | tf_op jit(solution)/shard_map/gather | solution.py:177
  272.2 3.0 %gather_fusion.1 = bf16[64,64,192]{2,1,0:T(8,128)(2,1)S(1)} fusion(bf16[128,64,192]{2,1,0:T(8,128)(2,1)} %bitcast.15, s32[1024]{0:T(1024)} %pad_clamp_fusion), kind=kCustom, calls=%fused_computation.1 | custom fusion | bytes 3145984 | tf_op jit(solution)/shard_map/gather | solution.py:176
  277.9 3.2 %fusion.41 = f32[4,512,128]{2,1,0:T(8,128)} fusion(bf16[4,1024,128]{2,1,0:T(8,128)(2,1)S(1)} %bitcast.120, f32[4,1024,512]{2,1,0:T(8,128)S(1)} %get-tuple-element.17, f32[4,512]{1,0:T(4,128)S(1)} %get-tuple-element.16, f32[4,512]{1,0:T(4,128)S(1)} %fusion.3), kind=kOutput, calls=%fused_computation.50 | convolution fusion | flops 543424512 | bytes 10502144 | tf_op jit(solution)/shard_map/dot_general | solution.py:38
  281.1 1.5 reshape_reshape.7
  283.7 1.9 fusion.39
  (154 shorter events, 46.8 us)
Async XLA Ops:
  6.5 25.1 %copy-start.7 = (bf16[1024,192]{0,1:T(8,128)(2,1)S(1)}, bf16[1024,192]{0,1:T(8,128)(2,1)}, u32[]{:S(2)}) copy-start(bf16[1024,192]{0,1:T(8,128)(2,1)} %param.10) | copy-start | bytes 1179652
  6.5 25.3 %copy-start.2 = (bf16[128,3072]{1,0:T(8,128)(2,1)S(1)}, bf16[128,3072]{1,0:T(8,128)(2,1)}, u32[]{:S(2)}) copy-start(bf16[128,3072]{1,0:T(8,128)(2,1)} %param.9) | copy-start | bytes 2359300
  6.5 61.4 %all-gather.5.cloned.1.call-start = ((), (), s32[]{:S(2)}) async-start(), calls=%async_computation.5 | async-start | bytes 1310720 | tf_op jit(solution)/shard_map/all_gather | solution.py:66
  10.3 28.1 %copy-start.18 = (bf16[16,192,3]{1,0,2:T(8,128)(2,1)S(1)}, bf16[16,192,3]{1,0,2:T(8,128)(2,1)}, u32[]{:S(2)}) copy-start(bf16[16,192,3]{1,0,2:T(8,128)(2,1)} %param.17) | copy-start | bytes 55300
  10.3 39.6 %collective-permute-start = (bf16[163840]{0:T(1024)(128)(2,1)}, bf16[163840]{0:T(1024)(128)(2,1)}, u32[]{:S(2)}, u32[]{:S(2)}) collective-permute-start(bf16[163840]{0:T(1024)(128)(2,1)} %pad_maximum_fusion.2), channel_id=1, source_target_pairs={{7,0},{0,1},{1,2},{2,3},{3,4},{4,5},{5,6},{6,7},{15,8},{8,9},{9,10... | collective-permute-start | bytes 983048 | tf_op jit(solution)/shard_map/ppermute | solution.py:15
  24.7 24.5 %all-to-all-start.1 = ((s32[8,1,16]{2,1,0:T(1,128)}), s32[8,1,16]{2,1,0:T(1,128)}, u32[]{:S(2)}, u32[]{:S(2)}) async-start(s32[8,1,16]{2,1,0:T(1,128)} %bitcast.11), calls=%async_computation.1 | async-start | bytes 8192 | tf_op jit(solution)/shard_map/all_to_all | solution.py:168
  30.8 9.3 %copy-start = (bf16[1024,128]{1,0:T(8,128)(2,1)S(1)}, bf16[1024,128]{1,0:T(8,128)(2,1)}, u32[]{:S(2)}) copy-start(bf16[1024,128]{1,0:T(8,128)(2,1)} %param.11) | copy-start | bytes 786436
  30.8 149.6 %all-gather.3.cloned.1.call-start = ((), (), s32[]{:S(2)}) async-start(), calls=%async_computation.4 | async-start | bytes 2949120 | tf_op jit(solution)/shard_map/all_gather | solution.py:65
  31.6 9.4 %copy-start.17 = (bf16[128,192]{0,1:T(8,128)(2,1)S(1)}, bf16[128,192]{0,1:T(8,128)(2,1)}, u32[]{:S(2)}) copy-start(bf16[128,192]{0,1:T(8,128)(2,1)} %param.12) | copy-start | bytes 147460
  41.1 0.8 copy-start.9
  42.4 23.7 %slice-start = ((bf16[1024,128]{1,0:T(8,128)(2,1)}), bf16[1008,128]{1,0:T(8,128)(2,1)S(1)}, s32[]{:S(2)}) async-start(bf16[1024,128]{1,0:T(8,128)(2,1)} %param.11), calls=%async_computation.6 | async-start | bytes 516096 | tf_op jit(solution)/shard_map/slice | solution.py:106
  52.5 56.1 %collective-permute-start.1 = (bf16[204800]{0:T(1024)(128)(2,1)}, bf16[204800]{0:T(1024)(128)(2,1)}, u32[]{:S(2)}, u32[]{:S(2)}) collective-permute-start(bf16[204800]{0:T(1024)(128)(2,1)} %pad_maximum_fusion), channel_id=1, source_target_pairs={{0,4},{1,5},{2,6},{3,7},{8,12},{9,13},{10,14},{11,15},{16,20},{17,... | collective-permute-start | bytes 1228808 | tf_op jit(solution)/shard_map/ppermute | solution.py:21
  57.1 51.5 %collective-permute-start.2 = (bf16[204800]{0:T(1024)(128)(2,1)}, bf16[204800]{0:T(1024)(128)(2,1)}, u32[]{:S(2)}, u32[]{:S(2)}) collective-permute-start(bf16[204800]{0:T(1024)(128)(2,1)} %pad_maximum_fusion), channel_id=1, source_target_pairs={{0,3},{1,4},{2,5},{3,6},{4,7},{8,11},{9,12},{10,13},{11,14},{12,15... | collective-permute-start | bytes 1228808 | tf_op jit(solution)/shard_map/ppermute | solution.py:21
  60.7 48.0 %collective-permute-start.3 = (bf16[204800]{0:T(1024)(128)(2,1)}, bf16[204800]{0:T(1024)(128)(2,1)}, u32[]{:S(2)}, u32[]{:S(2)}) collective-permute-start(bf16[204800]{0:T(1024)(128)(2,1)} %pad_maximum_fusion), channel_id=1, source_target_pairs={{0,2},{1,3},{2,4},{3,5},{4,6},{5,7},{8,10},{9,11},{10,12},{11,13},... | collective-permute-start | bytes 1228808 | tf_op jit(solution)/shard_map/ppermute | solution.py:21
  63.3 45.4 %collective-permute-start.4 = (bf16[204800]{0:T(1024)(128)(2,1)}, bf16[204800]{0:T(1024)(128)(2,1)}, u32[]{:S(2)}, u32[]{:S(2)}) collective-permute-start(bf16[204800]{0:T(1024)(128)(2,1)} %pad_maximum_fusion), channel_id=1, source_target_pairs={{0,1},{1,2},{2,3},{3,4},{4,5},{5,6},{6,7},{8,9},{9,10},{10,11},{11... | collective-permute-start | bytes 1228808 | tf_op jit(solution)/shard_map/ppermute | solution.py:21
  71.2 14.9 %all-to-all-start = ((bf16[8,64,128]{2,1,0:T(8,128)(2,1)}), bf16[8,64,128]{2,1,0:T(8,128)(2,1)}, u32[]{:S(2)}, u32[]{:S(2)}) async-start(bf16[8,64,128]{2,1,0:T(8,128)(2,1)} %stack.2), calls=%async_computation | async-start | bytes 262144 | tf_op jit(solution)/shard_map/all_to_all | solution.py:131
  75.4 2.8 copy-start.1
  86.1 71.7 %all-to-all-start.3 = ((bf16[8,16,64,128]{3,2,1,0:T(8,128)(2,1)}), bf16[8,16,64,128]{3,2,1,0:T(8,128)(2,1)}, u32[]{:S(2)}, u32[]{:S(2)}) async-start(bf16[8,16,64,128]{3,2,1,0:T(8,128)(2,1)} %bitcast.114), calls=%async_computation.3 | async-start | bytes 4194304 | tf_op jit(solution)/shard_map/all_to_all | solution.py:171
  157.8 13.3 %copy-start.16 = (bf16[128,128]{1,0:T(8,128)(2,1)S(1)}, bf16[128,128]{1,0:T(8,128)(2,1)}, u32[]{:S(2)}) copy-start(bf16[128,128]{1,0:T(8,128)(2,1)} %param.13) | copy-start | bytes 98308
  157.8 14.0 %copy-start.10 = (bf16[128,192]{1,0:T(8,128)(2,1)S(1)}, bf16[128,192]{1,0:T(8,128)(2,1)}, u32[]{:S(2)}) copy-start(bf16[128,192]{1,0:T(8,128)(2,1)} %copy-done.9) | copy-start | bytes 147460
  157.8 114.4 %all-to-all-start.2 = ((bf16[8,16,64,192]{3,2,1,0:T(8,128)(2,1)}), bf16[8,16,64,192]{3,2,1,0:T(8,128)(2,1)}, u32[]{:S(2)}, u32[]{:S(2)}) async-start(bf16[8,16,64,192]{3,2,1,0:T(8,128)(2,1)} %bitcast.111), calls=%async_computation.2 | async-start | bytes 8388608 | tf_op jit(solution)/shard_map/all_to_all | solution.py:170
  176.4 4.0 %copy-start.11 = (bf16[64,3072]{1,0:T(8,128)(2,1)S(1)}, bf16[64,3072]{1,0:T(8,128)(2,1)}, u32[]{:S(2)}) copy-start(bf16[64,3072]{1,0:T(8,128)(2,1)} %reshape.398) | copy-start | bytes 1179652
  176.4 5.8 %copy-start.12 = (bf16[64,3072]{1,0:T(8,128)(2,1)S(1)}, bf16[64,3072]{1,0:T(8,128)(2,1)}, u32[]{:S(2)}) copy-start(bf16[64,3072]{1,0:T(8,128)(2,1)} %reshape.397) | copy-start | bytes 1179652
  179.3 84.1 %copy-start.4 = (bf16[2048,192]{1,0:T(8,128)(2,1)S(1)}, bf16[2048,192]{1,0:T(8,128)(2,1)}, u32[]{:S(2)}) copy-start(bf16[2048,192]{1,0:T(8,128)(2,1)} %reshape.399) | copy-start | bytes 2359300
  179.3 84.1 %copy-start.19 = (pred[512]{0:T(512)(128)(4,1)S(1)}, pred[512]{0:T(512)(128)(4,1)}, u32[]{:S(2)}) copy-start(pred[512]{0:T(512)(128)(4,1)} %iota_compare_fusion.1) | copy-start | bytes 1540
  267.6 7.6 %copy-start.3 = (bf16[4,512,192]{2,1,0:T(8,128)(2,1)S(1)}, bf16[4,512,192]{2,1,0:T(8,128)(2,1)}, u32[]{:S(2)}) copy-start(bf16[4,512,192]{2,1,0:T(8,128)(2,1)} %reshape_reshape.6) | copy-start | bytes 2359300
  276.5 1.4 copy-start.8
  277.9 4.7 %copy-start.13 = (f32[128,16]{1,0:T(8,128)S(1)}, f32[128,16]{1,0:T(8,128)}, u32[]{:S(2)}) copy-start(f32[128,16]{1,0:T(8,128)} %copy.36) | copy-start | bytes 24580
  277.9 5.1 %copy-start.14 = (f32[128,16]{1,0:T(8,128)S(1)}, f32[128,16]{1,0:T(8,128)}, u32[]{:S(2)}) copy-start(f32[128,16]{1,0:T(8,128)} %copy.41) | copy-start | bytes 24580
  281.1 2.2 copy-start.15
  281.1 2.6 copy-start.5
  281.1 2.6 copy-start.6
Sparse Core Ops, SparseCore 0:
  9.2 29.2 all-gather.4
  40.3 37.3 all-gather.2
